TPU v7x, 512 devices: a whole 4x4x16 slice. The times are simulated.
512 devices in a mesh: seq: 16 (over y, x), mp: 32 (over z, core).
Axes of the slice: x: 4, y: 4, z: 16, core: 2. Of those that a mesh axis runs over, the one named last changes fastest.
Arguments:
- q_proj: bfloat16 [4096, 8192], P('seq', 'mp'), may hold values from -6 to 6
- k_proj: bfloat16 [4096, 8192], P('seq', 'mp'), may hold values from -6 to 6
- v_proj: bfloat16 [4096, 8192], P('seq', 'mp'), may hold values from -6 to 6
- out_grad: bfloat16 [4096, 8192], P('seq', 'mp'), may hold values from -0.75 to 0.75
- out_weight: bfloat16 [8192, 8192], P('mp', 'seq'), may hold values from -0.0625 to 0.0625
- taps: float32 [7, 512], P(None, 'mp'), may hold values from -2.4 to 2.4
Outputs:
- grad_q: bfloat16 [4096, 8192], P('seq', 'mp')
- grad_k: bfloat16 [4096, 8192], P('seq', 'mp')
- grad_v: bfloat16 [4096, 8192], P('seq', 'mp')
- grad_weight: float32 [8192, 8192], P('mp', 'seq')
- grad_taps: float32 [7, 512], P(None, 'mp')
All inputs are finite; a program needn't handle non-finite values.
Results may differ from a plain program's by a relative error of at most 0.0029.
Values may be sent and summed in bfloat16 or wider, within the bound.
A program may use at most 64 MiB of HBM per device.

v0:
```python
import functools

import jax
import jax.numpy as jnp
from jax import lax
from jax.experimental import pallas as pl
from jax.experimental.pallas import tpu as pltpu
from jax.sharding import PartitionSpec as P

TAPS = 7
GROUP = 16
PAD = 16
EDGE = 8
MESH = pl.DeviceIdType.MESH
F32 = jnp.float32
BF16 = jnp.bfloat16


def dot(a, b, dims):
    return lax.dot_general(a, b, ((dims[0:1], dims[1:2]), ((), ())), preferred_element_type=F32)


def exact_dot(a, b):
    return lax.dot_general(
        a,
        b,
        (((1,), (0,)), ((), ())),
        precision=lax.Precision.HIGHEST,
        preferred_element_type=F32,
    )


def kernel(
    side,
    q_ref, k_ref, v_ref, g_ref, w_ref, taps_ref,
    gq_ref, gk_ref, gv_ref, gw_ref, gt_ref,
    cols, gat, sent1, got1, own, sent2, got2, fin,
    k_edge, v_edge, prod, filt, gfil, spread, terms, terms_got,
    cross_s, cross_r, cross_l, edge_s, edge_r, ga_s, ga_r, gb_s, gb_r,
    ring_s, ring_r, core_s, core_r, one_s, one_r, two_s, two_r,
    back_s, back_r, term_s, term_r,
):
    n = side * side
    far = n // 2
    rows, chans = q_ref.shape
    half, wide = rows // 2, chans // 2
    s, m = lax.axis_index("seq"), lax.axis_index("mp")
    z, c = m // 2, m % 2
    y, x = s // side, s % side

    def ring(t):
        return lax.rem(t + 2 * n, n)

    def seq_dev(i):
        return (i, m)

    def at_xy(yy, xx):
        return (lax.rem(yy + side, side) * side + lax.rem(xx + side, side), m)

    def rc(src, dst, ss, rs, dev):
        return pltpu.make_async_remote_copy(
            src_ref=src, dst_ref=dst, send_sem=ss, recv_sem=rs, device_id=dev, device_id_type=MESH
        )

    crossed = (z, 2 * s + c)
    up, down = (s, 2 * ring(z + 1) + c), (s, 2 * ring(z - 1) + c)
    mate = (s, 2 * z + 1 - c)
    off_diagonal = s != z

    barrier = pltpu.get_barrier_semaphore()
    for d in range(1, n):
        pl.semaphore_signal(
            barrier, inc=1, device_id=seq_dev(ring(s + d)), device_id_type=MESH
        )
    for dev in (up, down, mate):
        pl.semaphore_signal(barrier, inc=1, device_id=dev, device_id_type=MESH)

    @pl.when(off_diagonal)
    def _():
        pl.semaphore_signal(barrier, inc=1, device_id=crossed, device_id_type=MESH)
        pl.semaphore_wait(barrier, n + 3)

    @pl.when(jnp.logical_not(off_diagonal))
    def _():
        pl.semaphore_wait(barrier, n + 2)

    def cross():
        return rc(g_ref, cols.at[c, s], cross_s.at[0], cross_r.at[0], crossed)

    def cross_in():
        return rc(g_ref, cols.at[c, z], cross_s.at[0], cross_r.at[0], crossed)

    def cross_local():
        return pltpu.make_async_copy(g_ref, cols.at[c, z], cross_l.at[0])

    @pl.when(off_diagonal)
    def _():
        cross().start()

    @pl.when(jnp.logical_not(off_diagonal))
    def _():
        cross_local().start()

    def edges(dev):
        tail = pl.ds(rows - PAD, PAD)
        return (
            rc(k_ref.at[tail], k_edge, edge_s.at[0], edge_r.at[0], seq_dev(dev)),
            rc(v_ref.at[tail], v_edge, edge_s.at[1], edge_r.at[1], seq_dev(dev)),
        )

    @pl.when(s < n - 1)
    def _():
        for copy in edges(s + 1):
            copy.start()

    group = lax.broadcasted_iota(jnp.int32, (GROUP, chans), 1) // GROUP
    lane = lax.broadcasted_iota(jnp.int32, (GROUP, chans), 0)
    spread[0:TAPS] = exact_dot(taps_ref[...], jnp.where(group == lane, 1.0, 0.0).astype(F32))
    prod[PAD:] = k_ref[...].astype(F32) * v_ref[...].astype(F32)

    @pl.when(s == 0)
    def _():
        prod[0:PAD] = jnp.zeros((PAD, chans), F32)

    @pl.when(s > 0)
    def _():
        for copy in edges(s - 1):
            copy.wait_recv()
        prod[0:PAD] = k_edge[...].astype(F32) * v_edge[...].astype(F32)

    total = jnp.zeros((rows, chans), F32)
    for o in range(TAPS):
        total = total + spread[o : o + 1] * prod[PAD - o : PAD - o + rows]
    filt[...] = total
    gated = (q_ref[...].astype(F32) * total).astype(BF16)
    gat[s, 0] = gated[:half]
    gat[s, 1] = gated[half:]

    def gather_a(h, d, sign):
        to = at_xy(y, x + d * sign) if h == 0 else at_xy(y + d * sign, x)
        block = s if sign > 0 else to[0]
        piece = gat.at[block, h]
        return rc(piece, piece, ga_s.at[h, d - 1], ga_r.at[h, d - 1], to)

    def gather_b(h, d, e, sign):
        if h == 0:
            block, to = at_xy(y, x - e)[0], at_xy(y + d * sign, x)
            came = at_xy(y - d, x - e)[0]
        else:
            block, to = at_xy(y - e, x)[0], at_xy(y, x + d * sign)
            came = at_xy(y - e, x - d)[0]
        piece = gat.at[block if sign > 0 else came, h]
        return rc(piece, piece, gb_s.at[h, d - 1, e], gb_r.at[h, d - 1, e], to)

    for d in range(1, side):
        for h in range(2):
            gather_a(h, d, 1).start()
    for h in range(2):
        for d in range(1, side):
            gather_b(h, d, 0, 1).start()
    for e in range(1, side):
        for h in range(2):
            gather_a(h, e, -1).wait_recv()
            for d in range(1, side):
                gather_b(h, d, e, 1).start()

    def hop(way, k, j, t):
        piece = cols.at[c, t, pl.ds(j * half, half)]
        sems = ring_s.at[way, k, j], ring_r.at[way, k, j]
        return rc(piece, piece, *sems, up if way == 0 else down)

    def share(t, which):
        piece = cols.at[which, t]
        return rc(piece, piece, core_s.at[t], core_r.at[t], mate)

    gw_ref[...] = jnp.zeros(gw_ref.shape, F32)

    @pl.when(off_diagonal)
    def _():
        cross_in().wait_recv()

    @pl.when(jnp.logical_not(off_diagonal))
    def _():
        cross_local().wait()

    for j in range(2):
        for way in range(2):
            if far > 1 or way == j:
                hop(way, 0, j, z).start()
    share(z, c).start()
    for h in range(2):
        for d in range(1, side):
            for e in range(side):
                gather_b(h, d, e, -1).wait_recv()

    def leg_one(h, t):
        ty, tx = t // side, t % side
        outer, inner, here = (ty, tx, x) if h == 0 else (tx, ty, y)
        d = lax.rem(inner - here + side, side)
        to = at_xy(y, tx) if h == 0 else at_xy(ty, x)
        return outer, d, to

    def one_copy(h, t, outer, d, to):
        return rc(
            sent1.at[h, t], got1.at[h, outer, d - 1],
            one_s.at[h, outer, d - 1], one_r.at[h, outer, d - 1], to,
        )

    def process(t):
        share(t, 1 - c).wait_recv()
        left, right = cols[0, t], cols[1, t]
        part = dot(left, w_ref[:, :chans], (1, 1)) + dot(right, w_ref[:, chans:], (1, 1))
        for h in range(2):
            outer, d, to = leg_one(h, t)
            piece = part[:, h * wide : (h + 1) * wide]

            @pl.when(d == 0)
            def _():
                own[h, outer] = piece

            @pl.when(d != 0)
            def _():
                sent1[h, t] = piece.astype(BF16)
                one_copy(h, t, outer, d, to).start()

        for j in range(2):
            near = gat[t, j]
            span = slice(j * half, (j + 1) * half)
            gw_ref[:, :chans] += dot(near, left[span], (0, 0))
            gw_ref[:, chans:] += dot(near, right[span], (0, 0))

    def leg_two(h, t):
        ty, tx = t // side, t % side
        outer, there = (ty, y) if h == 0 else (tx, x)
        d = lax.rem(outer - there + side, side)
        to = at_xy(ty, x) if h == 0 else at_xy(y, tx)
        return outer, d, to

    def two_copy(h, outer, d, to):
        return rc(
            sent2.at[h, outer], got2.at[h, d - 1], two_s.at[h, d - 1], two_r.at[h, d - 1], to
        )

    def finish(t):
        for h in range(2):
            _, d_one, _ = leg_one(h, t)
            outer, d, to = leg_two(h, t)

            @pl.when(d_one == 0)
            def _():
                acc = own[h, outer]
                for e in range(1, side):
                    one_copy(h, t, outer, e, at_xy(y, x - 1)).wait_recv()
                    acc = acc + got1[h, outer, e - 1].astype(F32)

                @pl.when(d == 0)
                def _():
                    fin[h] = acc

                @pl.when(d != 0)
                def _():
                    sent2[h, outer] = acc
                    two_copy(h, outer, d, to).start()

    def step(k, carry):
        a, b = ring(z - k), ring(z + k)

        @pl.when(k < far)
        def _():
            for j in range(2):
                for way, t in ((0, a), (1, b)):
                    hop(way, k - 1, j, t).wait_recv()
                    if way == j:
                        hop(way, k, j, t).start()
                    else:

                        @pl.when(k < far - 1)
                        def _():
                            hop(way, k, j, t).start()

            share(a, c).start()
            share(b, c).start()

        @pl.when(k == far)
        def _():
            for way in range(2):
                hop(way, far - 1, way, a).wait_recv()
            share(a, c).start()

        @pl.when(k <= far + 1)
        def _():
            process(ring(z - k + 1))

        @pl.when(jnp.logical_and(k > 1, k <= far))
        def _():
            process(ring(z + k - 1))

        @pl.when(k >= 3)
        def _():
            finish(ring(z - k + 3))

        @pl.when(jnp.logical_and(k > 3, k <= far + 2))
        def _():
            finish(ring(z + k - 3))

        return carry

    lax.fori_loop(1, far + 4, step, 0)

    for h in range(2):
        span = slice(h * wide, (h + 1) * wide)
        acc = fin[h]
        for d in range(1, side):
            two_copy(h, 0, d, at_xy(y, x - 1)).wait_recv()
            acc = acc + got2[h, d - 1]
        gq_ref[:, span] = (acc * filt[:, span]).astype(BF16)
        gfil[0:rows, span] = acc * q_ref[:, span].astype(F32)

    def back(dev):
        return rc(
            gfil.at[pl.ds(0, EDGE)], gfil.at[pl.ds(rows, EDGE)],
            back_s.at[0], back_r.at[0], seq_dev(dev),
        )

    @pl.when(s > 0)
    def _():
        back(s - 1).start()

    @pl.when(s == n - 1)
    def _():
        gfil[rows:] = jnp.zeros((EDGE, chans), F32)

    grad_filtered = gfil[0:rows]
    term_rows = [
        jnp.sum(grad_filtered * prod[PAD - o : PAD - o + rows], 0, keepdims=True)
        for o in range(TAPS)
    ]
    stacked = jnp.concatenate(term_rows + [jnp.zeros((1, chans), F32)], 0)
    lanes = terms.shape[1]
    group_t = lax.broadcasted_iota(jnp.int32, (chans, lanes), 0) // GROUP
    lane_t = lax.broadcasted_iota(jnp.int32, (chans, lanes), 1)
    terms[...] = exact_dot(stacked, jnp.where(group_t == lane_t, 1.0, 0.0).astype(F32))

    def term(d, dev):
        return rc(terms, terms_got.at[d - 1], term_s.at[d - 1], term_r.at[d - 1], seq_dev(dev))

    for d in range(1, n):
        term(d, ring(s + d)).start()

    @pl.when(s < n - 1)
    def _():
        back(s + 1).wait_recv()

    grad_product = jnp.zeros((rows, chans), F32)
    for o in range(TAPS):
        grad_product = grad_product + spread[o : o + 1] * gfil[o : o + rows]
    gk_ref[...] = (grad_product * v_ref[...].astype(F32)).astype(BF16)
    gv_ref[...] = (grad_product * k_ref[...].astype(F32)).astype(BF16)

    term_sum = terms[...]
    for d in range(1, n):
        term(d, ring(s - d)).wait_recv()
        term_sum = term_sum + terms_got[d - 1]
    gt_ref[...] = term_sum[0:TAPS, 0:GROUP]

    @pl.when(off_diagonal)
    def _():
        cross().wait_send()

    @pl.when(s < n - 1)
    def _():
        for copy in edges(s + 1):
            copy.wait_send()

    for h in range(2):
        for d in range(1, side):
            gather_a(h, d, 1).wait_send()
            for e in range(side):
                gather_b(h, d, e, 1).wait_send()

    def sent_hops(k, carry):
        for j in range(2):
            for way in range(2):
                if way == j:
                    hop(way, k, j, z).wait_send()
                else:

                    @pl.when(k < far - 1)
                    def _():
                        hop(way, k, j, z).wait_send()

        return carry

    lax.fori_loop(0, far, sent_hops, 0)

    def sent_shares(t, carry):
        share(t, c).wait_send()
        return carry

    lax.fori_loop(0, n, sent_shares, 0)

    def sent_sums(outer, carry):
        for h in range(2):
            for d in range(1, side):
                one_copy(h, 0, outer, d, at_xy(y, x - 1)).wait_send()
        return carry

    lax.fori_loop(0, side, sent_sums, 0)
    for h in range(2):
        for d in range(1, side):
            two_copy(h, 0, d, at_xy(y, x - 1)).wait_send()

    @pl.when(s > 0)
    def _():
        back(s - 1).wait_send()

    for d in range(1, n):
        term(d, ring(s + d)).wait_send()


def shards(side, q, k, v, g, w, taps):
    n = side * side
    rows, chans = q.shape
    half, wide = rows // 2, chans // 2
    vmem = pl.BlockSpec(memory_space=pltpu.VMEM)
    dma = pltpu.SemaphoreType.DMA
    sems = [
        (1,), (1,), (1,), (2,), (2,),
        (2, side - 1), (2, side - 1), (2, side - 1, side), (2, side - 1, side),
        (2, n // 2, 2), (2, n // 2, 2), (n,), (n,),
        (2, side, side - 1), (2, side, side - 1), (2, side - 1), (2, side - 1),
        (1,), (1,), (n - 1,), (n - 1,),
    ]
    return pl.pallas_call(
        functools.partial(kernel, side),
        out_shape=(
            jax.ShapeDtypeStruct((rows, chans), BF16),
            jax.ShapeDtypeStruct((rows, chans), BF16),
            jax.ShapeDtypeStruct((rows, chans), BF16),
            jax.ShapeDtypeStruct(w.shape, F32),
            jax.ShapeDtypeStruct(taps.shape, F32),
        ),
        in_specs=[vmem] * 6,
        out_specs=[vmem] * 5,
        scratch_shapes=[
            pltpu.VMEM((2, n, rows, chans), BF16),
            pltpu.VMEM((n, 2, half, chans), BF16),
            pltpu.VMEM((2, n, rows, wide), BF16),
            pltpu.VMEM((2, side, side - 1, rows, wide), BF16),
            pltpu.VMEM((2, side, rows, wide), F32),
            pltpu.VMEM((2, side, rows, wide), F32),
            pltpu.VMEM((2, side - 1, rows, wide), F32),
            pltpu.VMEM((2, rows, wide), F32),
            pltpu.VMEM((PAD, chans), BF16),
            pltpu.VMEM((PAD, chans), BF16),
            pltpu.VMEM((PAD + rows, chans), F32),
            pltpu.VMEM((rows, chans), F32),
            pltpu.VMEM((rows + EDGE, chans), F32),
            pltpu.VMEM((8, chans), F32),
            pltpu.VMEM((8, 128), F32),
            pltpu.VMEM((n - 1, 8, 128), F32),
        ]
        + [dma(shape) for shape in sems],
        compiler_params=pltpu.CompilerParams(
            collective_id=0, has_side_effects=True, vmem_limit_bytes=48 * 2**20
        ),
    )(q, k, v, g, w, taps)


def solution(mesh):
    side = int(round(mesh.shape["seq"] ** 0.5))
    tiles, weight, filters = P("seq", "mp"), P("mp", "seq"), P(None, "mp")
    return jax.shard_map(
        functools.partial(shards, side),
        mesh=mesh,
        in_specs=(tiles, tiles, tiles, tiles, weight, filters),
        out_specs=(tiles, tiles, tiles, weight, filters),
        check_vma=False,
    )
```

profile of v0, /device:TPU:64, one launch (start us, length us, event | category | flops | bytes accessed | tf_op | source)
XLA Modules:
  0.0 111.9 jit_solution(8116874201335636014)
XLA Ops:
  0.6 0.0 copy-start
  0.6 0.9 copy-done
  1.6 0.0 copy-start.1
  1.6 0.9 copy-done.1
  2.5 0.0 copy-start.2
  2.5 0.9 copy-done.2
  3.4 0.0 copy-start.3
  3.4 0.9 copy-done.3
  4.3 0.0 copy-start.4
  4.3 0.9 copy-done.4
  5.2 0.0 copy-start.5
  5.2 0.7 copy-done.5
  5.9 102.7 %shard_map.101 = (bf16[256,256]{1,0:T(8,128)(2,1)S(1)}, bf16[256,256]{1,0:T(8,128)(2,1)S(1)}, bf16[256,256]{1,0:T(8,128)(2,1)S(1)}, f32[256,512]{1,0:T(8,128)S(1)}, f32[7,16]{1,0:T(8,128)S(1)}) custom-call(bf16[256,256]{1,0:T(8,128)(2,1)S(1)} %copy-done.1, bf16[256,256]{1,0:T(8,128)(2,1)S(1)} %copy-done.2, bf16[256,256]{1,0:T(8,128)(2,1)S(1)} %copy-done.3, ...), custom_call_target="tpu_custom_call" | custom-call | tf_op jit(solution)/shard_map/pallas_call | solution.py:434
  108.6 0.7 copy.16
  109.2 0.7 copy.17
  109.9 0.7 copy.18
  110.5 0.8 copy.19
  111.3 0.6 copy.20
Async XLA Ops:
  0.6 1.0 copy-start
  1.6 0.9 copy-start.1
  2.5 0.9 copy-start.2
  3.4 0.9 copy-start.3
  4.3 0.9 copy-start.4
  5.2 0.7 copy-start.5
where the time goes:
time: 112 us
  Pallas kernels  103 us (92%)
  local copies, waits for them, and re-layouts  8.6 us (8%)
    pallas_call x1, Pallas kernels, shards(): pl.pallas_call(functools.partial(kernel, side), out_shape=(jax.ShapeDtype...  103 us
    unnamed x17, local copies, waits for them, and re-layouts  8.6 us

commit v1 on v0

--- a/solution.py
+++ b/solution.py
@@ -11,6 +11,7 @@
 GROUP = 16
 PAD = 16
 EDGE = 8
+PARTS = 4
 MESH = pl.DeviceIdType.MESH
 F32 = jnp.float32
 BF16 = jnp.bfloat16
@@ -32,24 +33,32 @@
 
 def kernel(
     side,
-    q_ref, k_ref, v_ref, g_ref, w_ref, taps_ref,
+    q_in, k_in, v_in, g_ref, w_in, taps_in,
     gq_ref, gk_ref, gv_ref, gw_ref, gt_ref,
     cols, gat, sent1, got1, own, sent2, got2, fin,
-    k_edge, v_edge, prod, filt, gfil, spread, terms, terms_got,
+    q_ref, k_ref, v_ref, w_ref, taps_ref, k_edge, v_edge, prod, filt, gfil, spread, terms, terms_got,
     cross_s, cross_r, cross_l, edge_s, edge_r, ga_s, ga_r, gb_s, gb_r,
     ring_s, ring_r, core_s, core_r, one_s, one_r, two_s, two_r,
-    back_s, back_r, term_s, term_r,
+    back_s, back_r, term_s, term_r, load_s,
 ):
     n = side * side
     far = n // 2
-    rows, chans = q_ref.shape
-    half, wide = rows // 2, chans // 2
+    rows, chans = q_in.shape
+    half, wide, slab = rows // 2, chans // 2, rows // PARTS
     s, m = lax.axis_index("seq"), lax.axis_index("mp")
     z, c = m // 2, m % 2
     y, x = s // side, s % side
+    loads = [
+        pltpu.make_async_copy(src, dst, load_s.at[i])
+        for i, (src, dst) in enumerate(
+            ((k_in, k_ref), (v_in, v_ref), (taps_in, taps_ref), (q_in, q_ref), (w_in, w_ref))
+        )
+    ]
+    for load in loads:
+        load.start()
 
     def ring(t):
-        return lax.rem(t + 2 * n, n)
+        return lax.rem(t + 4 * n, n)
 
     def seq_dev(i):
         return (i, m)
@@ -62,10 +71,16 @@
             src_ref=src, dst_ref=dst, send_sem=ss, recv_sem=rs, device_id=dev, device_id_type=MESH
         )
 
-    crossed = (z, 2 * s + c)
+
+    def skew(i):
+        return i + side * (i % side)
+
+    target = ring(s + skew(z))
+    crossed = (z, 2 * target + c)
+    source = (ring(z - skew(s)), 2 * s + c)
     up, down = (s, 2 * ring(z + 1) + c), (s, 2 * ring(z - 1) + c)
     mate = (s, 2 * z + 1 - c)
-    off_diagonal = s != z
+    off_diagonal = jnp.logical_or(s != z, target != z)
 
     barrier = pltpu.get_barrier_semaphore()
     for d in range(1, n):
@@ -77,7 +92,7 @@
 
     @pl.when(off_diagonal)
     def _():
-        pl.semaphore_signal(barrier, inc=1, device_id=crossed, device_id_type=MESH)
+        pl.semaphore_signal(barrier, inc=1, device_id=source, device_id_type=MESH)
         pl.semaphore_wait(barrier, n + 3)
 
     @pl.when(jnp.logical_not(off_diagonal))
@@ -85,7 +100,7 @@
         pl.semaphore_wait(barrier, n + 2)
 
     def cross():
-        return rc(g_ref, cols.at[c, s], cross_s.at[0], cross_r.at[0], crossed)
+        return rc(g_ref, cols.at[c, target], cross_s.at[0], cross_r.at[0], crossed)
 
     def cross_in():
         return rc(g_ref, cols.at[c, z], cross_s.at[0], cross_r.at[0], crossed)
@@ -104,8 +119,8 @@
     def edges(dev):
         tail = pl.ds(rows - PAD, PAD)
         return (
-            rc(k_ref.at[tail], k_edge, edge_s.at[0], edge_r.at[0], seq_dev(dev)),
-            rc(v_ref.at[tail], v_edge, edge_s.at[1], edge_r.at[1], seq_dev(dev)),
+            rc(k_in.at[tail], k_edge, edge_s.at[0], edge_r.at[0], seq_dev(dev)),
+            rc(v_in.at[tail], v_edge, edge_s.at[1], edge_r.at[1], seq_dev(dev)),
         )
 
     @pl.when(s < n - 1)
@@ -113,6 +128,8 @@
         for copy in edges(s + 1):
             copy.start()
 
+    for load in loads:
+        load.wait()
     group = lax.broadcasted_iota(jnp.int32, (GROUP, chans), 1) // GROUP
     lane = lax.broadcasted_iota(jnp.int32, (GROUP, chans), 0)
     spread[0:TAPS] = exact_dot(taps_ref[...], jnp.where(group == lane, 1.0, 0.0).astype(F32))
@@ -133,13 +150,12 @@
         total = total + spread[o : o + 1] * prod[PAD - o : PAD - o + rows]
     filt[...] = total
     gated = (q_ref[...].astype(F32) * total).astype(BF16)
-    gat[s, 0] = gated[:half]
-    gat[s, 1] = gated[half:]
+    gat[s] = gated
 
     def gather_a(h, d, sign):
         to = at_xy(y, x + d * sign) if h == 0 else at_xy(y + d * sign, x)
         block = s if sign > 0 else to[0]
-        piece = gat.at[block, h]
+        piece = gat.at[block, pl.ds(h * half, half)]
         return rc(piece, piece, ga_s.at[h, d - 1], ga_r.at[h, d - 1], to)
 
     def gather_b(h, d, e, sign):
@@ -149,7 +165,7 @@
         else:
             block, to = at_xy(y - e, x)[0], at_xy(y, x + d * sign)
             came = at_xy(y - e, x - d)[0]
-        piece = gat.at[block if sign > 0 else came, h]
+        piece = gat.at[block if sign > 0 else came, pl.ds(h * half, half)]
         return rc(piece, piece, gb_s.at[h, d - 1, e], gb_r.at[h, d - 1, e], to)
 
     for d in range(1, side):
@@ -165,7 +181,7 @@
                 gather_b(h, d, e, 1).start()
 
     def hop(way, k, j, t):
-        piece = cols.at[c, t, pl.ds(j * half, half)]
+        piece = cols.at[c, t, pl.ds(j * slab, slab)]
         sems = ring_s.at[way, k, j], ring_r.at[way, k, j]
         return rc(piece, piece, *sems, up if way == 0 else down)
 
@@ -173,8 +189,6 @@
         piece = cols.at[which, t]
         return rc(piece, piece, core_s.at[t], core_r.at[t], mate)
 
-    gw_ref[...] = jnp.zeros(gw_ref.shape, F32)
-
     @pl.when(off_diagonal)
     def _():
         cross_in().wait_recv()
@@ -183,15 +197,13 @@
     def _():
         cross_local().wait()
 
-    for j in range(2):
+    for j in range(PARTS):
         for way in range(2):
-            if far > 1 or way == j:
-                hop(way, 0, j, z).start()
+            hop(way, 0, j, z).start()
     share(z, c).start()
-    for h in range(2):
-        for d in range(1, side):
-            for e in range(side):
-                gather_b(h, d, e, -1).wait_recv()
+
+    def last_way(j):
+        return 2 * j // PARTS
 
     def leg_one(h, t):
         ty, tx = t // side, t % side
@@ -206,10 +218,10 @@
             one_s.at[h, outer, d - 1], one_r.at[h, outer, d - 1], to,
         )
 
-    def process(t):
-        share(t, 1 - c).wait_recv()
-        left, right = cols[0, t], cols[1, t]
-        part = dot(left, w_ref[:, :chans], (1, 1)) + dot(right, w_ref[:, chans:], (1, 1))
+    def process(p):
+        t = ring(p - skew(s))
+        share(p, 1 - c).wait_recv()
+        part = dot(cols[0, p], w_ref[:, :chans], (1, 1)) + dot(cols[1, p], w_ref[:, chans:], (1, 1))
         for h in range(2):
             outer, d, to = leg_one(h, t)
             piece = part[:, h * wide : (h + 1) * wide]
@@ -223,89 +235,80 @@
                 sent1[h, t] = piece.astype(BF16)
                 one_copy(h, t, outer, d, to).start()
 
-        for j in range(2):
-            near = gat[t, j]
-            span = slice(j * half, (j + 1) * half)
-            gw_ref[:, :chans] += dot(near, left[span], (0, 0))
-            gw_ref[:, chans:] += dot(near, right[span], (0, 0))
-
-    def leg_two(h, t):
-        ty, tx = t // side, t % side
-        outer, there = (ty, y) if h == 0 else (tx, x)
-        d = lax.rem(outer - there + side, side)
-        to = at_xy(ty, x) if h == 0 else at_xy(y, tx)
-        return outer, d, to
-
     def two_copy(h, outer, d, to):
         return rc(
             sent2.at[h, outer], got2.at[h, d - 1], two_s.at[h, d - 1], two_r.at[h, d - 1], to
         )
 
-    def finish(t):
-        for h in range(2):
-            _, d_one, _ = leg_one(h, t)
-            outer, d, to = leg_two(h, t)
-
-            @pl.when(d_one == 0)
-            def _():
-                acc = own[h, outer]
-                for e in range(1, side):
-                    one_copy(h, t, outer, e, at_xy(y, x - 1)).wait_recv()
-                    acc = acc + got1[h, outer, e - 1].astype(F32)
-
-                @pl.when(d == 0)
-                def _():
-                    fin[h] = acc
-
-                @pl.when(d != 0)
-                def _():
-                    sent2[h, outer] = acc
-                    two_copy(h, outer, d, to).start()
-
     def step(k, carry):
         a, b = ring(z - k), ring(z + k)
 
+        def pass_on(j):
+            @pl.when(k < far)
+            def _():
+                for way, p in ((0, a), (1, b)):
+                    hop(way, k - 1, j, p).wait_recv()
+                    if way == last_way(j):
+                        hop(way, k, j, p).start()
+                    else:
+
+                        @pl.when(k < far - 1)
+                        def _():
+                            hop(way, k, j, p).start()
+
+            @pl.when(k == far)
+            def _():
+                hop(last_way(j), far - 1, j, a).wait_recv()
+
+        for j in range(PARTS // 2):
+            pass_on(j)
+        process(ring(z - k + 1))
+        for j in range(PARTS // 2, PARTS):
+            pass_on(j)
+
+        @pl.when(k <= far)
+        def _():
+            share(a, c).start()
+
         @pl.when(k < far)
         def _():
-            for j in range(2):
-                for way, t in ((0, a), (1, b)):
-                    hop(way, k - 1, j, t).wait_recv()
-                    if way == j:
-                        hop(way, k, j, t).start()
-                    else:
-
-                        @pl.when(k < far - 1)
-                        def _():
-                            hop(way, k, j, t).start()
-
-            share(a, c).start()
             share(b, c).start()
-
-        @pl.when(k == far)
-        def _():
-            for way in range(2):
-                hop(way, far - 1, way, a).wait_recv()
-            share(a, c).start()
-
-        @pl.when(k <= far + 1)
-        def _():
-            process(ring(z - k + 1))
 
         @pl.when(jnp.logical_and(k > 1, k <= far))
         def _():
             process(ring(z + k - 1))
 
-        @pl.when(k >= 3)
-        def _():
-            finish(ring(z - k + 3))
-
-        @pl.when(jnp.logical_and(k > 3, k <= far + 2))
-        def _():
-            finish(ring(z + k - 3))
-
         return carry
 
-    lax.fori_loop(1, far + 4, step, 0)
+    lax.fori_loop(1, far + 2, step, 0)
+
+    for i in range(1, side + 1):
+        d = i % side
+        for h in range(2):
+            outer = lax.rem((y if h == 0 else x) + i, side)
+            acc = own[h, outer]
+            for e in range(1, side):
+                one_copy(h, 0, outer, e, at_xy(y, x - 1)).wait_recv()
+                acc = acc + got1[h, outer, e - 1].astype(F32)
+            if d:
+                sent2[h, outer] = acc
+                two_copy(h, outer, d, at_xy(y + d, x) if h == 0 else at_xy(y, x + d)).start()
+            else:
+                fin[h] = acc
+
+    for h in range(2):
+        for d in range(1, side):
+            for e in range(side):
+                gather_b(h, d, e, -1).wait_recv()
+    gw_ref[...] = jnp.zeros(gw_ref.shape, F32)
+
+    def weigh(p, carry):
+        near = gat[ring(p - skew(s))]
+        gw_ref[:, :chans] += dot(near, cols[0, p], (0, 0))
+        gw_ref[:, chans:] += dot(near, cols[1, p], (0, 0))
+        return carry
+
+    lax.fori_loop(0, n, weigh, 0)
 
     for h in range(2):
         span = slice(h * wide, (h + 1) * wide)
@@ -379,9 +382,9 @@
                 gather_b(h, d, e, 1).wait_send()
 
     def sent_hops(k, carry):
-        for j in range(2):
+        for j in range(PARTS):
             for way in range(2):
-                if way == j:
+                if way == last_way(j):
                     hop(way, k, j, z).wait_send()
                 else:
 
@@ -421,15 +424,15 @@
 def shards(side, q, k, v, g, w, taps):
     n = side * side
     rows, chans = q.shape
-    half, wide = rows // 2, chans // 2
+    wide = chans // 2
     vmem = pl.BlockSpec(memory_space=pltpu.VMEM)
     dma = pltpu.SemaphoreType.DMA
     sems = [
         (1,), (1,), (1,), (2,), (2,),
         (2, side - 1), (2, side - 1), (2, side - 1, side), (2, side - 1, side),
-        (2, n // 2, 2), (2, n // 2, 2), (n,), (n,),
+        (2, n // 2, PARTS), (2, n // 2, PARTS), (n,), (n,),
         (2, side, side - 1), (2, side, side - 1), (2, side - 1), (2, side - 1),
-        (1,), (1,), (n - 1,), (n - 1,),
+        (1,), (1,), (n - 1,), (n - 1,), (5,),
     ]
     return pl.pallas_call(
         functools.partial(kernel, side),
@@ -440,17 +443,22 @@
             jax.ShapeDtypeStruct(w.shape, F32),
             jax.ShapeDtypeStruct(taps.shape, F32),
         ),
-        in_specs=[vmem] * 6,
+        in_specs=[pl.BlockSpec(memory_space=pltpu.HBM)] * 6,
         out_specs=[vmem] * 5,
         scratch_shapes=[
             pltpu.VMEM((2, n, rows, chans), BF16),
-            pltpu.VMEM((n, 2, half, chans), BF16),
+            pltpu.VMEM((n, rows, chans), BF16),
             pltpu.VMEM((2, n, rows, wide), BF16),
             pltpu.VMEM((2, side, side - 1, rows, wide), BF16),
             pltpu.VMEM((2, side, rows, wide), F32),
             pltpu.VMEM((2, side, rows, wide), F32),
             pltpu.VMEM((2, side - 1, rows, wide), F32),
             pltpu.VMEM((2, rows, wide), F32),
+            pltpu.VMEM((rows, chans), BF16),
+            pltpu.VMEM((rows, chans), BF16),
+            pltpu.VMEM((rows, chans), BF16),
+            pltpu.VMEM(w.shape, BF16),
+            pltpu.VMEM(taps.shape, F32),
             pltpu.VMEM((PAD, chans), BF16),
             pltpu.VMEM((PAD, chans), BF16),
             pltpu.VMEM((PAD + rows, chans), F32),
@@ -462,7 +470,7 @@
         ]
         + [dma(shape) for shape in sems],
         compiler_params=pltpu.CompilerParams(
-            collective_id=0, has_side_effects=True, vmem_limit_bytes=48 * 2**20
+            collective_id=0, has_side_effects=True, vmem_limit_bytes=63 * 2**20
         ),
     )(q, k, v, g, w, taps)
 

time: 112 us -> 89.9 us (0.80)
  the two profiles are of different devices: /device:TPU:64 before, /device:TPU:96 now
where the time goes in v1:
time: 89.9 us; the launch traced here: 89.8 us
  Pallas kernels  83 us (92%)
  local copies, waits for them, and re-layouts  6.15 us (7%)
    pallas_call x1, Pallas kernels, shards(): pl.pallas_call(functools.partial(kernel, side), out_shape=(jax.ShapeDtype...  83 us
    unnamed x9, local copies, waits for them, and re-layouts  6.15 us

profile of v1, /device:TPU:96, one launch (start us, length us, event | category | flops | bytes accessed | tf_op | source)
XLA Modules:
  0.0 89.8 jit_solution(6421345037425306403)
XLA Ops:
  0.6 83.0 %shard_map.101 = (bf16[256,256]{1,0:T(8,128)(2,1)}, bf16[256,256]{1,0:T(8,128)(2,1)}, bf16[256,256]{1,0:T(8,128)(2,1)}, f32[256,512]{1,0:T(8,128)}, f32[7,16]{1,0:T(8,128)}) custom-call(bf16[256,256]{1,0:T(8,128)(2,1)} %q_in.1, bf16[256,256]{1,0:T(8,128)(2,1)} %k_in.1, bf16[256,256]{1,0:T(8,128)(2,1)} %v_in.1, bf16[256,256]{1,0:T(8,128)(2,1)} %g_ref.1, ...), custom_call_target="tpu_custom_call" | custom-call | tf_op jit(solution)/shard_map/pallas_call | solution.py:437
  83.6 0.0 copy-start
  83.6 1.6 %copy.16 = bf16[256,256]{1,0:T(8,128)(2,1)} copy(bf16[256,256]{1,0:T(8,128)(2,1)} %get-tuple-element.10) | data formatting | bytes 262144
  85.2 1.6 %copy.17 = bf16[256,256]{1,0:T(8,128)(2,1)} copy(bf16[256,256]{1,0:T(8,128)(2,1)} %get-tuple-element.11) | data formatting | bytes 262144
  86.8 1.6 %copy.18 = bf16[256,256]{1,0:T(8,128)(2,1)} copy(bf16[256,256]{1,0:T(8,128)(2,1)} %get-tuple-element.12) | data formatting | bytes 262144
  88.4 0.0 copy-done
  88.4 0.0 copy-start.1
  88.4 0.8 copy.19
  89.2 0.0 copy-done.1
  89.2 0.6 copy.20
Async XLA Ops:
  83.6 4.8 %copy-start = (f32[256,512]{1,0:T(8,128)S(1)}, f32[256,512]{1,0:T(8,128)}, u32[]{:S(2)}) copy-start(f32[256,512]{1,0:T(8,128)} %get-tuple-element.13) | copy-start | bytes 1572868
  88.4 0.8 copy-start.1

commit v2 on v1

--- a/solution.py
+++ b/solution.py
@@ -93,40 +93,6 @@
     @pl.when(off_diagonal)
     def _():
         pl.semaphore_signal(barrier, inc=1, device_id=source, device_id_type=MESH)
-        pl.semaphore_wait(barrier, n + 3)
-
-    @pl.when(jnp.logical_not(off_diagonal))
-    def _():
-        pl.semaphore_wait(barrier, n + 2)
-
-    def cross():
-        return rc(g_ref, cols.at[c, target], cross_s.at[0], cross_r.at[0], crossed)
-
-    def cross_in():
-        return rc(g_ref, cols.at[c, z], cross_s.at[0], cross_r.at[0], crossed)
-
-    def cross_local():
-        return pltpu.make_async_copy(g_ref, cols.at[c, z], cross_l.at[0])
-
-    @pl.when(off_diagonal)
-    def _():
-        cross().start()
-
-    @pl.when(jnp.logical_not(off_diagonal))
-    def _():
-        cross_local().start()
-
-    def edges(dev):
-        tail = pl.ds(rows - PAD, PAD)
-        return (
-            rc(k_in.at[tail], k_edge, edge_s.at[0], edge_r.at[0], seq_dev(dev)),
-            rc(v_in.at[tail], v_edge, edge_s.at[1], edge_r.at[1], seq_dev(dev)),
-        )
-
-    @pl.when(s < n - 1)
-    def _():
-        for copy in edges(s + 1):
-            copy.start()
 
     for load in loads:
         load.wait()
@@ -135,6 +101,49 @@
     spread[0:TAPS] = exact_dot(taps_ref[...], jnp.where(group == lane, 1.0, 0.0).astype(F32))
     prod[PAD:] = k_ref[...].astype(F32) * v_ref[...].astype(F32)
 
+    total = jnp.zeros((rows - PAD, chans), F32)
+    for o in range(TAPS):
+        total = total + spread[o : o + 1] * prod[2 * PAD - o : PAD - o + rows]
+    filt[PAD:] = total
+
+    @pl.when(off_diagonal)
+    def _():
+        pl.semaphore_wait(barrier, n + 3)
+
+    @pl.when(jnp.logical_not(off_diagonal))
+    def _():
+        pl.semaphore_wait(barrier, n + 2)
+
+    def cross():
+        return rc(g_ref, cols.at[c, target], cross_s.at[0], cross_r.at[0], crossed)
+
+    def cross_in():
+        return rc(g_ref, cols.at[c, z], cross_s.at[0], cross_r.at[0], crossed)
+
+    def cross_local():
+        return pltpu.make_async_copy(g_ref, cols.at[c, z], cross_l.at[0])
+
+    @pl.when(off_diagonal)
+    def _():
+        cross().start()
+
+    @pl.when(jnp.logical_not(off_diagonal))
+    def _():
+        cross_local().start()
+
+    def edges(dev):
+        tail = pl.ds(rows - PAD, PAD)
+        return (
+            rc(k_in.at[tail], k_edge, edge_s.at[0], edge_r.at[0], seq_dev(dev)),
+            rc(v_in.at[tail], v_edge, edge_s.at[1], edge_r.at[1], seq_dev(dev)),
+        )
+
+    @pl.when(s < n - 1)
+    def _():
+        for copy in edges(s + 1):
+            copy.start()
+
+
     @pl.when(s == 0)
     def _():
         prod[0:PAD] = jnp.zeros((PAD, chans), F32)
@@ -145,11 +154,11 @@
             copy.wait_recv()
         prod[0:PAD] = k_edge[...].astype(F32) * v_edge[...].astype(F32)
 
-    total = jnp.zeros((rows, chans), F32)
+    first = jnp.zeros((PAD, chans), F32)
     for o in range(TAPS):
-        total = total + spread[o : o + 1] * prod[PAD - o : PAD - o + rows]
-    filt[...] = total
-    gated = (q_ref[...].astype(F32) * total).astype(BF16)
+        first = first + spread[o : o + 1] * prod[PAD - o : 2 * PAD - o]
+    filt[0:PAD] = first
+    gated = (q_ref[...].astype(F32) * filt[...]).astype(BF16)
     gat[s] = gated
 
     def gather_a(h, d, sign):
@@ -421,6 +430,19 @@
         term(d, ring(s + d)).wait_send()
 
 
+def write_out(*refs):
+    results, outs, held, sems = refs[0:5], refs[5:10], refs[10:15], refs[15]
+    loads = [pltpu.make_async_copy(results[i], held[i], sems.at[0, i]) for i in range(5)]
+    stores = [pltpu.make_async_copy(held[i], outs[i], sems.at[1, i]) for i in range(5)]
+    for load in loads:
+        load.start()
+    for load, store in zip(loads, stores):
+        load.wait()
+        store.start()
+    for store in stores:
+        store.wait()
+
+
 def shards(side, q, k, v, g, w, taps):
     n = side * side
     rows, chans = q.shape
@@ -434,7 +456,7 @@
         (2, side, side - 1), (2, side, side - 1), (2, side - 1), (2, side - 1),
         (1,), (1,), (n - 1,), (n - 1,), (5,),
     ]
-    return pl.pallas_call(
+    results = pl.pallas_call(
         functools.partial(kernel, side),
         out_shape=(
             jax.ShapeDtypeStruct((rows, chans), BF16),
@@ -473,6 +495,14 @@
             collective_id=0, has_side_effects=True, vmem_limit_bytes=63 * 2**20
         ),
     )(q, k, v, g, w, taps)
+    return pl.pallas_call(
+        write_out,
+        out_shape=tuple(jax.ShapeDtypeStruct(r.shape, r.dtype) for r in results),
+        in_specs=[pl.BlockSpec(memory_space=pltpu.HBM)] * 5,
+        out_specs=[pl.BlockSpec(memory_space=pltpu.HBM)] * 5,
+        scratch_shapes=[pltpu.VMEM(r.shape, r.dtype) for r in results] + [dma((2, 5))],
+        compiler_params=pltpu.CompilerParams(vmem_limit_bytes=63 * 2**20),
+    )(*results)
 
 
 def solution(mesh):

time: 89.9 us -> 86 us (0.957)
  local copies, waits for them, and re-layouts: 6.15 us -> 0 us
  Pallas kernels: 83 us -> 85.1 us
    unnamed x9 -> x0, local copies, waits for them, and re-layouts: 6.15 us -> none
    pallas_call x0 -> x1, Pallas kernels: none -> 2.13 us  [shards(): pl.pallas_call(write_out, out_shape=tuple((jax.ShapeDtypeStruct(r.shape,...]
where the time goes in v2:
time: 86 us; the launch traced here: 85.8 us
  Pallas kernels  85.1 us (99%)
    pallas_call x1, Pallas kernels, shards(): pl.pallas_call(functools.partial(kernel, side), out_shape=(jax.ShapeDtype...  83 us
    pallas_call x1, Pallas kernels, shards(): pl.pallas_call(write_out, out_shape=tuple((jax.ShapeDtypeStruct(r.shape,...  2.13 us

profile of v2, /device:TPU:96, one launch (start us, length us, event | category | flops | bytes accessed | tf_op | source)
XLA Modules:
  0.0 85.8 jit_solution(16380482515273377604)
XLA Ops:
  0.6 83.0 %shard_map.101 = (bf16[256,256]{1,0:T(8,128)(2,1)}, bf16[256,256]{1,0:T(8,128)(2,1)}, bf16[256,256]{1,0:T(8,128)(2,1)}, f32[256,512]{1,0:T(8,128)}, f32[7,16]{1,0:T(8,128)}) custom-call(bf16[256,256]{1,0:T(8,128)(2,1)} %q_in.1, bf16[256,256]{1,0:T(8,128)(2,1)} %k_in.1, bf16[256,256]{1,0:T(8,128)(2,1)} %v_in.1, bf16[256,256]{1,0:T(8,128)(2,1)} %g_ref.1, ...), custom_call_target="tpu_custom_call" | custom-call | tf_op jit(solution)/shard_map/pallas_call | solution.py:459
  83.7 2.1 %shard_map.102 = (bf16[256,256]{1,0:T(8,128)(2,1)}, bf16[256,256]{1,0:T(8,128)(2,1)}, bf16[256,256]{1,0:T(8,128)(2,1)}, f32[256,512]{1,0:T(8,128)}, f32[7,16]{1,0:T(8,128)}) custom-call(bf16[256,256]{1,0:T(8,128)(2,1)} %get-tuple-element.10.refs_0_, bf16[256,256]{1,0:T(8,128)(2,1)} %get-tuple-element.11.refs_1_, bf16[256,256]{1,0:T(8,128)(2,1)} %get-tuple-element.12.refs_2_, ...), custom_call_target="tpu_custom_call" | custom-call | tf_op jit(solution)/shard_map/pallas_call | solution.py:498

commit v3 on v2

--- a/solution.py
+++ b/solution.py
@@ -325,7 +325,7 @@
         for d in range(1, side):
             two_copy(h, 0, d, at_xy(y, x - 1)).wait_recv()
             acc = acc + got2[h, d - 1]
-        gq_ref[:, span] = (acc * filt[:, span]).astype(BF16)
+        fin[h] = acc
         gfil[0:rows, span] = acc * q_ref[:, span].astype(F32)
 
     def back(dev):
@@ -358,6 +358,10 @@
 
     for d in range(1, n):
         term(d, ring(s + d)).start()
+
+    for h in range(2):
+        span = slice(h * wide, (h + 1) * wide)
+        gq_ref[:, span] = (fin[h] * filt[:, span]).astype(BF16)
 
     @pl.when(s < n - 1)
     def _():

time: 86 us -> 85.9 us (level)
  no operation moved by 1% of the time
where the time goes in v3:
time: 85.9 us; the launch traced here: 85.8 us
  Pallas kernels  85.1 us (99%)
    pallas_call x1, Pallas kernels, shards(): pl.pallas_call(functools.partial(kernel, side), out_shape=(jax.ShapeDtype...  83 us
    pallas_call x1, Pallas kernels, shards(): pl.pallas_call(write_out, out_shape=tuple((jax.ShapeDtypeStruct(r.shape,...  2.13 us

profile of v3, /device:TPU:96, one launch (start us, length us, event | category | flops | bytes accessed | tf_op | source)
XLA Modules:
  0.0 85.8 jit_solution(902060919279848730)
XLA Ops:
  0.6 83.0 %shard_map.101 = (bf16[256,256]{1,0:T(8,128)(2,1)}, bf16[256,256]{1,0:T(8,128)(2,1)}, bf16[256,256]{1,0:T(8,128)(2,1)}, f32[256,512]{1,0:T(8,128)}, f32[7,16]{1,0:T(8,128)}) custom-call(bf16[256,256]{1,0:T(8,128)(2,1)} %q_in.1, bf16[256,256]{1,0:T(8,128)(2,1)} %k_in.1, bf16[256,256]{1,0:T(8,128)(2,1)} %v_in.1, bf16[256,256]{1,0:T(8,128)(2,1)} %g_ref.1, ...), custom_call_target="tpu_custom_call" | custom-call | tf_op jit(solution)/shard_map/pallas_call | solution.py:463
  83.6 2.1 %shard_map.102 = (bf16[256,256]{1,0:T(8,128)(2,1)}, bf16[256,256]{1,0:T(8,128)(2,1)}, bf16[256,256]{1,0:T(8,128)(2,1)}, f32[256,512]{1,0:T(8,128)}, f32[7,16]{1,0:T(8,128)}) custom-call(bf16[256,256]{1,0:T(8,128)(2,1)} %get-tuple-element.10.refs_0_, bf16[256,256]{1,0:T(8,128)(2,1)} %get-tuple-element.11.refs_1_, bf16[256,256]{1,0:T(8,128)(2,1)} %get-tuple-element.12.refs_2_, ...), custom_call_target="tpu_custom_call" | custom-call | tf_op jit(solution)/shard_map/pallas_call | solution.py:502
